TPU v7x, 128 devices: a whole 4x4x4 slice. The times are simulated.
128 devices in a mesh: dp: 4 (over y), grid: 32 (over z, x, core).
Axes of the slice: x: 4, y: 4, z: 4, core: 2. Of those that a mesh axis runs over, the one named last changes fastest.
Arguments:
- unembed_feature_matrix: bfloat16 [16, 131072, 512], P('dp', 'grid'), may hold values from -6 to 6
- weight_in: bfloat16 [512, 512], replicated, may hold values from -0.25 to 0.25
- bias_in: float32 [512], replicated, may hold values from -3 to 3
- readout_weight: bfloat16 [512], replicated, may hold values from -0.25 to 0.25
- measured_rainfall: float32 [16, 131072], P('dp', 'grid'), may hold values from -20 to 20
- land_mask: int32 [131072], P('grid'), may hold values 0 or 1
- morton: int32 [32, 4096], P('grid'), may hold values from 0 to 4095, each once within a row
Outputs:
- predicted_rainfall: float32 [16, 131072], P('dp', 'grid')
- patch_prediction_deriv: float32 [16, 131072], P('dp', 'grid')
- penalty_per_example: float32 [16], P('dp')
- inner_coefficient_deriv: float32 [512, 512], P('grid')
- offset_projection_derivs: float32 [2, 512], replicated
Inputs may be any that keep to these rules, and one draw needn't show every extreme that they name: `morton`: each row is a permutation of 0 to 4095.
All inputs are finite; a program needn't handle non-finite values. No bound on the sum of `land_mask` on one device may be relied on, other than what follows from the above.
Results may differ from a plain program's by a relative error of at most 0.0029.
Values sent between devices are 32-bit elements; how exact they have to be, the bound alone decides.
No kernel may reach another device: no remote copies, remote signals or barrier semaphores. Data moves between devices by JAX's collectives and lax.ppermute only.
A program may use at most 192 MiB of HBM per device.

v0:
```python
import jax
import jax.numpy as jnp
from jax import lax
from jax.sharding import PartitionSpec as P

sharpness = 0.5


def swapped(block, axis, distance):
    count = lax.axis_size(axis)
    route = []
    for low in range(count):
        high = low | 1 << distance
        if high != low and high < count:
            route += [(low, high), (high, low)]
    return lax.ppermute(block, axis, route)


def smooth_abs(value):
    return jnp.sqrt(1.0 + value * value) - 1.0


def smooth_slope(value):
    return value / jnp.sqrt(1.0 + value * value)


def on_device(
    unembed_feature_matrix, weight_in, bias_in, readout_weight, measured_rainfall, land_mask, morton
):
    example_total, patch_total, width = unembed_feature_matrix.shape
    tiles = lax.axis_size("grid")
    grad_scale = (width / (example_total * lax.axis_size("dp") * patch_total * tiles)) ** 0.5
    flat_rows = unembed_feature_matrix.reshape(example_total * patch_total, width)
    preact = jnp.dot(flat_rows, weight_in, preferred_element_type=jnp.float32) + bias_in
    logistic = jax.nn.sigmoid(preact)
    hidden_activation = (preact * logistic).astype(jnp.bfloat16)
    predicted_rainfall = jnp.dot(
        hidden_activation, readout_weight, preferred_element_type=jnp.float32
    ).reshape(example_total, patch_total)
    patch_penalty_factor = 1.0 + land_mask.astype(jnp.float32)
    prediction_residual = patch_penalty_factor * (predicted_rainfall - measured_rainfall)
    zorder_line = morton[0]
    sorted_entries = jnp.take(prediction_residual, zorder_line, axis=1)
    steepness = jnp.zeros((example_total, patch_total), jnp.float32)
    loss_local = jnp.zeros((example_total,), jnp.float32)
    node_cells = 1
    while node_cells <= patch_total:
        grouped = sorted_entries.reshape(example_total, patch_total // node_cells, node_cells)
        means = jnp.sum(grouped, axis=2) / node_cells
        loss_local = loss_local + node_cells * jnp.sum(smooth_abs(sharpness * means), axis=1)
        steepness = steepness + jnp.repeat(smooth_slope(sharpness * means), node_cells, axis=1)
        node_cells = node_cells * 4
    tile_total = jnp.sum(sorted_entries, axis=1)
    coarse_slope = jnp.zeros((example_total,), jnp.float32)
    bit_count = tiles.bit_length() - 1
    running = tile_total
    for bit_number in range(bit_count):
        running = running + swapped(running, "grid", bit_number)
        if bit_number % 2 == 1 or bit_number == bit_count - 1:
            group = 2 ** (bit_number + 1)
            means = running / (group * patch_total)
            loss_local = loss_local + patch_total * smooth_abs(sharpness * means)
            coarse_slope = coarse_slope + smooth_slope(sharpness * means)
    steepness = steepness + coarse_slope[:, None]
    penalty_per_example = lax.psum(loss_local, "grid") / (patch_total * tiles * sharpness)
    patch_prediction_deriv = (
        jnp.zeros_like(steepness).at[:, zorder_line].set(steepness) * patch_penalty_factor
    )
    derivative_vector = patch_prediction_deriv.reshape(example_total * patch_total)
    epilogue = (
        derivative_vector[:, None]
        * readout_weight.astype(jnp.float32)
        * (logistic * (1.0 + preact * (1.0 - logistic)))
    ).astype(jnp.bfloat16)
    bias_term = jnp.sum(epilogue.astype(jnp.float32), axis=0)
    out_term = jnp.sum(derivative_vector[:, None] * hidden_activation, axis=0)
    vector_term = grad_scale * jnp.stack([bias_term, out_term])
    kept = width // tiles
    weight_term = grad_scale * lax.dot_general(
        flat_rows, epilogue, (((0,), (0,)), ((), ())), preferred_element_type=jnp.float32
    )
    summed, offset_projection_derivs = lax.psum((weight_term, vector_term), ("dp", "grid"))
    inner_coefficient_deriv = lax.dynamic_slice_in_dim(
        summed, lax.axis_index("grid") * kept, kept, 0
    )
    return (
        predicted_rainfall,
        patch_prediction_deriv,
        penalty_per_example,
        inner_coefficient_deriv,
        offset_projection_derivs,
    )


def solution(mesh):
    placed = (P("dp", "grid", None), P(), P(), P(), P("dp", "grid"), P("grid"), P("grid", None))
    return jax.shard_map(
        on_device,
        mesh=mesh,
        in_specs=placed,
        out_specs=(P("dp", "grid"), P("dp", "grid"), P("dp"), P("grid", None), P()),
        check_vma=False,
    )
```

profile of v0, /device:TPU:0, one launch (start us, length us, event | category | flops | bytes accessed | tf_op | source)
XLA Modules:
  0.0 325.3 jit_solution(12811384271982417352)
XLA Ops:
  7.2 0.0 copy-start
  7.2 0.0 all-reduce.2.cloned.1.call-start
  7.2 0.7 reshape.178
  8.0 0.3 copy-done
  8.2 29.1 %multiply_convert_fusion.1 = (bf16[16384,512]{1,0:T(8,128)(2,1)}, f32[16384,512]{1,0:T(8,128)}) fusion(f32[512]{0:T(512)} %param.9, bf16[16384,512]{1,0:T(8,128)(2,1)} %bitcast.84, bf16[512,512]{1,0:T(8,128)(2,1)S(1)} %copy-done), kind=kOutput, calls=%fused_computation.5 | convolution fusion | flops 8640266240 | bytes 67635200 | tf_op jit(solution)/shard_map/dot_general | solution.py:34
  37.3 10.2 %fusion.14 = f32[1,16384]{1,0:T(1,128)S(1)} fusion(bf16[16384,512]{1,0:T(8,128)(2,1)} %get-tuple-element.43, bf16[512,1]{0,1:T(2,128)(2,1)S(1)} %reshape.178), kind=kOutput, calls=%fused_computation.73 | convolution fusion | flops 16777216 | bytes 16843776 | tf_op jit(solution)/shard_map/dot_general | solution.py:37
  47.6 0.0 copy-done.2
  47.6 0.0 copy-start.3
  47.6 0.0 copy-start.6
  47.6 0.6 copy.29
  48.3 0.1 copy-done.5
  48.4 2.0 copy.30
  50.3 0.0 copy-done.3
  50.3 0.0 copy-done.6
  50.4 2.9 subtract_multiply_fusion
  53.3 12.4 %gather_fusion = f32[4096,4]{1,0:T(8,128)S(1)} fusion(f32[4,4096]{0,1:T(8,128)} %subtract_multiply_fusion, s32[4096]{0:T(1024)S(1)} %broadcast_clamp_fusion), kind=kCustom, calls=%fused_computation | custom fusion | bytes 147456 | tf_op jit(solution)/shard_map/jit(_take)/gather | solution.py:43
  65.7 0.0 copy-start.7
  65.7 2.3 add_reduce_fusion
  67.9 0.3 collective-permute-start
  68.2 0.1 squeeze.19
  68.3 0.1 squeeze.18
  68.4 2.2 fusion
  70.6 0.0 copy-done.7
  70.6 0.5 broadcast.295
  71.1 0.7 reduce.12
  71.8 0.5 squeeze.17
  72.3 0.2 compare_and_fusion
  72.5 5.9 %select_reduce_fusion.4 = f32[4,1024]{0,1:T(8,128)S(1)} fusion(f32[4,1024,4]{0,2,1:T(4,128)S(1)} %bitcast.70, pred[1024,4]{1,0:T(8,128)(4,1)S(1)} %compare_and_fusion), kind=kLoop, calls=%fused_computation.23 | loop fusion | flops 28672 | bytes 86016 | tf_op jit(solution)/shard_map/reduce_sum | solution.py:49
  78.4 0.2 copy.31
  78.5 0.1 add_reduce_fusion.1
  78.7 0.2 copy.32
  78.9 0.8 select_reduce_fusion
  79.8 0.7 select_reduce_fusion.1
  80.6 0.7 select_reduce_fusion.2
  81.3 0.1 copy.35
  81.4 0.1 add_reduce_fusion.5
  81.5 1.6 select_reduce_fusion.3
  83.2 0.1 copy.33
  83.2 0.1 add_reduce_fusion.3
  83.4 0.1 copy.36
  83.5 0.1 copy.34
  83.6 0.0 collective-permute-done
  83.6 1.7 collective-permute-start.1
  85.3 2.0 collective-permute-done.1
  87.3 3.1 collective-permute-start.2
  90.4 1.9 collective-permute-done.2
  92.4 2.0 collective-permute-start.3
  94.4 1.5 collective-permute-done.3
  95.9 4.0 %collective-permute-start.4 = (f32[4]{0:T(128)S(1)}, f32[4]{0:T(128)S(1)}, u32[]{:S(2)}, u32[]{:S(2)}) collective-permute-start(f32[4]{0:T(128)S(1)} %add.245), channel_id=1, source_target_pairs={{0,16},{16,0},{1,17},{17,1},{2,18},{18,2},{3,19},{19,3},{4,20},{20... | collective-permute-start | bytes 56 | tf_op jit(solution)/shard_map/ppermute | solution.py:16
  99.9 1.5 collective-permute-done.4
  101.5 0.4 broadcast_in_dim.64
  101.9 3.0 fusion.4
  104.8 11.8 %scatter_custom_fusion = f32[4,4096]{0,1:T(8,128)S(1)} fusion(s32[4096]{0:T(1024)S(1)} %bitcast.81, f32[4,4096]{0,1:T(8,128)} %fusion.4, f32[]{:T(128)} %constant.37.clone.1), kind=kCustom, calls=%fused_computation.9 | custom fusion | bytes 131076 | tf_op jit(solution)/shard_map/scatter | solution.py:67
  116.6 1.9 broadcast_multiply_fusion
  118.6 2.2 copy.38
  120.8 28.0 %convert_reduce_fusion = (f32[512]{0:T(512)S(1)}, bf16[16384,512]{1,0:T(8,128)(2,1)}, f32[512]{0:T(512)S(1)}) fusion(f32[16384,512]{1,0:T(8,128)} %get-tuple-element.44, f32[512]{0:T(512)S(1)} %copy-done.8, f32[512]{0:T(512)S(1)} %convert_element_type.20, f32[16384]{0:T(1024)S(1)} %bitcast.78, bf16[16384,512]{1,0:T(8,128)(2,1)} %get-tuple-element.43), kind=kLoop, calls=%fused_computation.3 | loop fusion | flops 134216704 | bytes 67182592 | tf_op jit(solution)/shard_map/reduce_sum | solution.py:75
  148.8 18.1 %fusion.7 = f32[512,512]{0,1:T(8,128)} fusion(bf16[16384,512]{1,0:T(8,128)(2,1)} %get-tuple-element.28, bf16[16384,512]{1,0:T(8,128)(2,1)} %bitcast.85), kind=kOutput, calls=%fused_computation.30 | convolution fusion | flops 8590196736 | bytes 34603008 | tf_op jit(solution)/shard_map/dot_general | solution.py:79
  166.9 0.0 all-reduce.2.cloned.1.call-update
  166.9 64.0 %psum.21 = f32[4]{0:T(128)S(1)} all-reduce(f32[4]{0:T(128)S(1)} %get-tuple-element.40), channel_id=1, replica_groups=mesh['dp'=4,'grid'=32] {'grid'}, use_global_device_ids=true, to_apply=%region_14.15 | all-reduce | flops 4 | bytes 32 | tf_op jit(solution)/shard_map/psum | solution.py:65
  231.0 64.6 %psum.23 = f32[2,512]{1,0:T(2,128)} all-reduce(f32[2,512]{1,0:T(2,128)S(1)} %maximum_multiply_fusion), channel_id=1, replica_groups=mesh['dp'=4,'grid'=32] {'dp','grid'}, use_global_device_ids=true, to_apply=%region_18.19 | all-reduce | flops 1024 | bytes 8192 | tf_op jit(solution)/shard_map/psum | solution.py:82
  295.6 0.5 broadcast_multiply_fusion.1
  296.1 20.6 %all-reduce.2.cloned.1.call-done = f32[512,512]{0,1:T(8,128)} async-done(((f32[512,512]{0,1:T(8,128)}), f32[512,512]{0,1:T(8,128)}) %all-reduce.2.cloned.1.call-update) | async-done | bytes 1048592 | tf_op jit(solution)/shard_map/psum | solution.py:82
  316.7 1.1 constant_dynamic-slice_fusion
  317.8 0.7 copy.39
  (29 shorter events, 0.3 us)
Async XLA Ops:
  7.2 1.1 copy-start
  7.2 309.5 %all-reduce.2.cloned.1.call-start = ((), (), s32[]{:S(2)}) async-start(), calls=%async_computation | async-start | bytes 2097152 | tf_op jit(solution)/shard_map/psum | solution.py:82
  37.3 10.2 %copy-start.2 = (s32[1,4096]{1,0:T(1,128)S(1)}, s32[1,4096]{1,0:T(1,128)}, u32[]{:S(2)}) copy-start(s32[1,4096]{1,0:T(1,128)} %param.13) | copy-start | bytes 49156
  47.5 0.9 copy-start.5
  47.6 2.8 copy-start.3
  47.6 2.7 copy-start.6
  65.7 4.9 %copy-start.7 = (bf16[512]{0:T(512)(128)(2,1)S(1)}, bf16[512]{0:T(512)(128)(2,1)}, u32[]{:S(2)}) copy-start(bf16[512]{0:T(512)(128)(2,1)} %param.10) | copy-start | bytes 3076
  67.9 15.7 %collective-permute-start = (f32[4]{0:T(128)S(1)}, f32[4]{0:T(128)S(1)}, u32[]{:S(2)}, u32[]{:S(2)}) collective-permute-start(f32[4]{0:T(128)S(1)} %get-tuple-element.26), channel_id=1, source_target_pairs={{0,1},{1,0},{2,3},{3,2},{4,5},{5,4},{6,7},{7,6},{8,9},{9,8},{10,11... | collective-permute-start | bytes 56 | tf_op jit(solution)/shard_map/ppermute | solution.py:16
  83.6 3.6 %collective-permute-start.1 = (f32[4]{0:T(128)S(1)}, f32[4]{0:T(128)S(1)}, u32[]{:S(2)}, u32[]{:S(2)}) collective-permute-start(f32[4]{0:T(128)S(1)} %add.241), channel_id=1, source_target_pairs={{0,2},{2,0},{1,3},{3,1},{4,6},{6,4},{5,7},{7,5},{8,10},{10,8},{9,1... | collective-permute-start | bytes 56 | tf_op jit(solution)/shard_map/ppermute | solution.py:16
  87.3 5.1 %collective-permute-start.2 = (f32[4]{0:T(128)S(1)}, f32[4]{0:T(128)S(1)}, u32[]{:S(2)}, u32[]{:S(2)}) collective-permute-start(f32[4]{0:T(128)S(1)} %add.242), channel_id=1, source_target_pairs={{0,4},{4,0},{1,5},{5,1},{2,6},{6,2},{3,7},{7,3},{8,12},{12,8},{9,1... | collective-permute-start | bytes 56 | tf_op jit(solution)/shard_map/ppermute | solution.py:16
  92.4 3.6 %collective-permute-start.3 = (f32[4]{0:T(128)S(1)}, f32[4]{0:T(128)S(1)}, u32[]{:S(2)}, u32[]{:S(2)}) collective-permute-start(f32[4]{0:T(128)S(1)} %add.244), channel_id=1, source_target_pairs={{0,8},{8,0},{1,9},{9,1},{2,10},{10,2},{3,11},{11,3},{4,12},{12,4},... | collective-permute-start | bytes 56 | tf_op jit(solution)/shard_map/ppermute | solution.py:16
  95.9 5.5 %collective-permute-start.4 = (f32[4]{0:T(128)S(1)}, f32[4]{0:T(128)S(1)}, u32[]{:S(2)}, u32[]{:S(2)}) collective-permute-start(f32[4]{0:T(128)S(1)} %add.245), channel_id=1, source_target_pairs={{0,16},{16,0},{1,17},{17,1},{2,18},{18,2},{3,19},{19,3},{4,20},{20... | collective-permute-start | bytes 56 | tf_op jit(solution)/shard_map/ppermute | solution.py:16
  118.6 2.2 copy-start.8
  120.8 28.0 %copy-start.4 = (f32[4,4096]{1,0:T(4,128)}, f32[4,4096]{1,0:T(4,128)S(1)}, u32[]{:S(2)}) copy-start(f32[4,4096]{1,0:T(4,128)S(1)} %copy.38) | copy-start | bytes 196612
  148.8 169.7 %copy-start.1 = (bf16[512,512]{1,0:T(8,128)(2,1)S(1)}, bf16[512,512]{1,0:T(8,128)(2,1)}, u32[]{:S(2)}) copy-start(bf16[512,512]{1,0:T(8,128)(2,1)} %param.8) | copy-start | bytes 1572868
Sparse Core Ops, SparseCore 0:
  167.0 149.5 all-reduce.1
where the time goes:
time: 327 us; the launch traced here: 325 us
  blocking collectives  129 us (39%)
  matrix products  57.4 us (18%)
  other arithmetic  51.9 us (16%)
  local copies, waits for them, and re-layouts  34.3 us (10%)
  waiting for transfers between devices  27.6 us (8%)
  between operations  14.3 us (4%)
  starting transfers between devices  11.1 us (3%)
    psum x1, blocking collectives, on_device(): lax.psum((weight_term, vector_term), ('dp', 'grid'))  64.6 us
    psum x1, blocking collectives, on_device(): lax.psum(loss_local, 'grid') / (patch_total * tiles * sharpness)  64 us
    dot_general x1, matrix products, on_device(): jnp.dot(flat_rows, weight_in, preferred_element_type=jnp.float32) + bias_in  29.1 us
    reduce_sum x1, other arithmetic, on_device(): bias_term = jnp.sum(epilogue.astype(jnp.float32), axis=0)  28 us
    psum x1, waiting for transfers between devices, on_device(): lax.psum((weight_term, vector_term), ('dp', 'grid'))  20.6 us
    dot_general x1, matrix products, on_device(): lax.dot_general(flat_rows, epilogue, (((0,), (0,)), ((), ())), preferred_...  18.1 us
    gather x1, local copies, waits for them, and re-layouts, on_device(): sorted_entries = jnp.take(prediction_residual, zorder_line, axis=1)  12.4 us
    reduce_sum x6, other arithmetic, on_device(): means = jnp.sum(grouped, axis=2) / node_cells  11.9 us
  transfers between devices with their start and end apart: 6, of which 5 were waited for; matrix products, arithmetic and copies ran while one was open for 5% of the time, Pallas kernels for 0%

commit v1 on v0

v1 whole, which is shorter than its diff:
```python
import functools

import jax
import jax.numpy as jnp
from jax import lax
from jax.experimental import pallas as pl
from jax.experimental.pallas import tpu as pltpu
from jax.sharding import Mesh, PartitionSpec as P

F32 = jnp.float32
BF16 = jnp.bfloat16
SHARP = 0.5
LANES = 128
CB = 256
VMEM_LIMIT = 56 << 20


def nt_dot(a, b):
    return lax.dot_general(a, b, (((1,), (1,)), ((), ())), preferred_element_type=F32)


def columns(row, count):
    return jnp.broadcast_to(row, (LANES, count)).T


def smooth_pair(v):
    root = jnp.sqrt(1.0 + v * v)
    return v * v / (1.0 + root), v / root


def load_weights(w_ref, b_ref, r_ref, wt_ref, bcol_ref, rcol_ref):
    width = w_ref.shape[0]
    wt_ref[...] = (0.5 * w_ref[...].astype(F32)).T.astype(BF16)
    bcol_ref[...] = columns(0.5 * b_ref[...], width)
    rcol_ref[...] = columns(r_ref[...].astype(F32), width)


def forward_kernel(
    x_ref, w_ref, b_ref, r_ref, meas_ref, land_ref,
    pred_ref, mm_ref, tot_ref,
    wt_ref, bcol_ref, rcol_ref, z_ref,
):
    step = pl.program_id(0)
    samples = x_ref.shape[0]
    rows = mm_ref.shape[0] // samples

    @pl.when(step == 0)
    def _():
        load_weights(w_ref, b_ref, r_ref, wt_ref, bcol_ref, rcol_ref)

    wt = wt_ref[...]
    width = wt.shape[0]
    bcol = bcol_ref
    rcol = rcol_ref

    def matmul(s):
        z_ref[s] = nt_dot(wt, x_ref[s])

    def elementwise(s):
        for k in range(CB // LANES):
            lane = pl.ds(k * LANES, LANES)
            part = jnp.zeros((8, LANES), F32)
            for u in range(0, width, 64):
                z = z_ref[s, u:u + 64, k * LANES:(k + 1) * LANES] + bcol[u:u + 64, :]
                act = z + z * jnp.tanh(z)
                act = act.astype(BF16).astype(F32) * rcol[u:u + 64, :]
                part = part + jnp.sum(act.reshape(8, 8, LANES), axis=0)
            pred = jnp.sum(part, axis=0, keepdims=True)
            pred_ref[s:s + 1, lane] = pred
            scale = 1.0 + land_ref[:, lane].astype(F32)
            row = s * rows + step * (CB // LANES) + k
            mm_ref[pl.ds(row, 1), :] = scale * (pred - meas_ref[s:s + 1, lane])

    matmul(0)
    for s in range(samples):
        if s + 1 < samples:
            matmul(s + 1)
        elementwise(s)

    @pl.when(step == pl.num_programs(0) - 1)
    def _():
        spot = lax.broadcasted_iota(jnp.int32, (1, LANES), 1)
        total = jnp.zeros((1, LANES), F32)
        for s in range(samples):
            value = jnp.sum(mm_ref[s * rows:(s + 1) * rows, :])
            total = total + jnp.where(spot == s, value, 0.0)
        tot_ref[...] = total


def tree_kernel(mm_ref, morton_ref, slope_ref, loss_ref):
    rows = morton_ref.shape[0]
    samples = mm_ref.shape[0] // rows
    total = samples * rows
    cells = rows * LANES
    place = morton_ref[...]
    high = lax.shift_right_logical(place, 7)
    low = jnp.bitwise_and(place, LANES - 1)

    pieces = []
    for s in range(samples):
        for v in range(0, rows, 8):
            hi_v = high[v:v + 8, :]
            lo_v = low[v:v + 8, :]
            out = jnp.zeros((8, LANES), F32)
            for h in range(rows):
                source = jnp.broadcast_to(mm_ref[s * rows + h:s * rows + h + 1, :], (8, LANES))
                out = jnp.where(hi_v == h, jnp.take_along_axis(source, lo_v, axis=1), out)
            pieces.append(out)
    entries = jnp.concatenate(pieces, axis=0)

    lane = lax.broadcasted_iota(jnp.int32, (total, LANES), 1)
    row = lax.broadcasted_iota(jnp.int32, (total, LANES), 0)

    def pair_lane(value, bit):
        other = jnp.where(
            jnp.bitwise_and(lane, bit) == 0,
            pltpu.roll(value, LANES - bit, 1),
            pltpu.roll(value, bit, 1),
        )
        return value + other

    def pair_row(value, bit):
        other = jnp.where(
            jnp.bitwise_and(row, bit) == 0,
            pltpu.roll(value, total - bit, 0),
            pltpu.roll(value, bit, 0),
        )
        return value + other

    loss, slope = smooth_pair(SHARP * entries)
    sums = entries
    node = 1
    while node < cells:
        for bit in (node, 2 * node):
            if bit < LANES:
                sums = pair_lane(sums, bit)
            else:
                sums = pair_row(sums, bit // LANES)
        node = node * 4
        more_loss, more_slope = smooth_pair((SHARP / node) * sums)
        loss = loss + more_loss
        slope = slope + more_slope

    spot = lax.broadcasted_iota(jnp.int32, (1, LANES), 1)
    loss_row = jnp.zeros((1, LANES), F32)
    for s in range(samples):
        value = jnp.sum(loss[s * rows:(s + 1) * rows, :])
        loss_row = loss_row + jnp.where(spot == s, value, 0.0)
    loss_ref[...] = loss_row

    first = slope.astype(BF16).astype(F32)
    rest = slope - first
    second = rest.astype(BF16).astype(F32)
    third = rest - second
    parts = (first, second, third)
    level = lax.broadcasted_iota(jnp.int32, (rows, LANES), 0)
    spread = lax.broadcasted_iota(jnp.int32, (LANES, LANES), 0)
    placed = jnp.zeros((3 * total, LANES), F32)
    for a in range(0, rows, 2):
        left, right = [], []
        for r in (a, a + 1):
            hit = level == high[r:r + 1, :]
            left.append(jnp.concatenate([
                jnp.where(hit, part[s * rows + r:s * rows + r + 1, :], 0.0)
                for part in parts for s in range(samples)
            ], axis=0))
            right.append(jnp.where(spread == low[r:r + 1, :], 1.0, 0.0))
        placed = placed + nt_dot(
            jnp.concatenate(left, axis=1).astype(BF16),
            jnp.concatenate(right, axis=1).astype(BF16),
        )
    slope_ref[...] = placed[:total] + (placed[total:2 * total] + placed[2 * total:])


def backward_kernel(
    spot_ref, x_ref, w_ref, b_ref, r_ref, slope_ref, land_ref, pairs_ref, loss_ref,
    deriv_ref, keep_ref, send_ref,
    wt_ref, bcol_ref, rcol_ref, coarse_ref, z_ref, e_ref, acc_ref, bias_ref, outp_ref, line_ref,
    *, groups, grad_scale,
):
    step = pl.program_id(0)
    samples = x_ref.shape[0]
    rows = slope_ref.shape[0] // samples
    cells = rows * LANES
    my_z, my_x, my_y, my_c = (spot_ref[n] for n in range(4))
    lane = lax.broadcasted_iota(jnp.int32, (1, LANES), 1)

    @pl.when(step == 0)
    def _():
        load_weights(w_ref, b_ref, r_ref, wt_ref, bcol_ref, rcol_ref)
        acc_ref[...] = jnp.zeros_like(acc_ref)
        bias_ref[...] = jnp.zeros_like(bias_ref)
        outp_ref[...] = jnp.zeros_like(outp_ref)
        pairs = pairs_ref[...]
        index = lax.broadcasted_iota(jnp.int32, pairs.shape, 0)
        mine = my_z * 4 + my_x
        slope = jnp.zeros((1, LANES), F32)
        loss = loss_ref[...]
        for group in groups:
            span = group // 2
            base = mine - lax.rem(mine, span)
            inside = jnp.logical_and(index >= base, index < base + span)
            total = jnp.sum(jnp.where(inside, pairs, 0.0), axis=0, keepdims=True)
            more_loss, more_slope = smooth_pair((SHARP / (group * cells)) * total)
            loss = loss + cells * more_loss
            slope = slope + more_slope
        for s in range(samples):
            value = jnp.sum(jnp.where(lane == s, slope, 0.0))
            coarse_ref[s:s + 1, :] = jnp.broadcast_to(value, (1, LANES))
        own = jnp.logical_and(lane >= my_y * samples, lane < (my_y + 1) * samples)
        line_ref[8:9, :] = jnp.where(own, pltpu.roll(loss, my_y * samples, 1), 0.0)
        line_ref[9:16, :] = jnp.zeros((7, LANES), F32)

    wt = wt_ref[...]
    width = wt.shape[0]

    def matmul(s):
        z_ref[s] = nt_dot(wt, x_ref[s])

    def gradient(s, k):
        row = step * (CB // LANES) + k
        scale = 1.0 + land_ref[pl.ds(row, 1), :].astype(F32)
        local = slope_ref[pl.ds(s * rows + row, 1), :]
        return (local + coarse_ref[s:s + 1, :]) * scale

    def elementwise(s):
        for k in range(CB // LANES):
            span = slice(k * LANES, (k + 1) * LANES)
            grad = gradient(s, k)
            deriv_ref[s:s + 1, span] = grad
            grad8 = jnp.broadcast_to(grad, (8, LANES))
            half8 = 0.5 * grad8
            for u in range(0, width, 64):
                z = z_ref[s, u:u + 64, span] + bcol_ref[u:u + 64, :]
                gate = 1.0 + jnp.tanh(z)
                act = z * gate
                bend = (1.0 + (z + z)) - act
                left = (rcol_ref[u:u + 64, :].reshape(8, 8, LANES) * half8).reshape(64, LANES)
                e = left * (gate * bend)
                e_ref[u:u + 64, s * CB + k * LANES:s * CB + (k + 1) * LANES] = e.astype(BF16)
                bias_ref[u:u + 64, :] += e
                act = act.astype(BF16).astype(F32)
                outp_ref[u:u + 64, :] += (act.reshape(8, 8, LANES) * grad8).reshape(64, LANES)

    matmul(0)
    for s in range(samples):
        if s + 1 < samples:
            matmul(s + 1)
        elementwise(s)
    acc_ref[...] += jnp.dot(
        e_ref[...], x_ref[...].reshape(samples * CB, width), preferred_element_type=F32
    )

    @pl.when(step == pl.num_programs(0) - 1)
    def _():
        acc_ref[...] = (acc_ref[...] * grad_scale).T
        bias = jnp.sum(bias_ref[...].T, axis=0, keepdims=True) * grad_scale
        outp = jnp.sum(outp_ref[...].T, axis=0, keepdims=True) * grad_scale
        for j in range(width // LANES):
            line_ref[j:j + 1, :] = bias[:, j * LANES:(j + 1) * LANES]
            line_ref[4 + j:5 + j, :] = outp[:, j * LANES:(j + 1) * LANES]
        for half, out in ((my_c, keep_ref), (1 - my_c, send_ref)):
            for slot in range(16):
                first = pl.multiple_of(16 * (2 * slot + half), 16)
                for j in range(width // LANES):
                    out[slot * 64 + j * 16:slot * 64 + (j + 1) * 16, :] = acc_ref[
                        pl.ds(first, 16), j * LANES:(j + 1) * LANES
                    ]
            out[1024:1040, :] = line_ref[...]


def whole(shape):
    return pl.BlockSpec(shape, lambda *_: (0,) * len(shape))


def on_device(
    unembed_feature_matrix, weight_in, bias_in, readout_weight, measured_rainfall, land_mask, morton
):
    samples, cells, width = unembed_feature_matrix.shape
    rows = cells // LANES
    tiles = lax.axis_size("z") * lax.axis_size("x") * lax.axis_size("c")
    grad_scale = (width / (samples * lax.axis_size("y") * cells * tiles)) ** 0.5
    steps = cells // CB
    bias_row = bias_in.reshape(1, width)
    readout_row = readout_weight.reshape(1, width)
    land_row = land_mask.reshape(1, cells)
    land_tile = land_mask.reshape(rows, LANES)
    params = pltpu.CompilerParams(
        dimension_semantics=("arbitrary",), vmem_limit_bytes=VMEM_LIMIT
    )
    weight_scratch = [
        pltpu.VMEM((width, width), BF16),
        pltpu.VMEM((width, LANES), F32),
        pltpu.VMEM((width, LANES), F32),
    ]
    x_spec = pl.BlockSpec((samples, CB, width), lambda i: (0, i, 0))
    row_spec = pl.BlockSpec((samples, CB), lambda i: (0, i))

    predicted_rainfall, mismatch, totals = pl.pallas_call(
        forward_kernel,
        grid=(steps,),
        in_specs=[
            x_spec, whole((width, width)), whole((1, width)), whole((1, width)), row_spec,
            pl.BlockSpec((1, CB), lambda i: (0, i)),
        ],
        out_specs=[row_spec, whole((samples * rows, LANES)), whole((1, LANES))],
        out_shape=[
            jax.ShapeDtypeStruct((samples, cells), F32),
            jax.ShapeDtypeStruct((samples * rows, LANES), F32),
            jax.ShapeDtypeStruct((1, LANES), F32),
        ],
        scratch_shapes=weight_scratch + [pltpu.VMEM((samples, width, CB), F32)],
        compiler_params=params,
        name="forward",
    )(unembed_feature_matrix, weight_in, bias_row, readout_row, measured_rainfall, land_row)

    core_pair = totals + lax.ppermute(totals, "c", [(0, 1), (1, 0)])
    pairs = lax.all_to_all(jnp.broadcast_to(core_pair, (16, LANES)), ("z", "x"), 0, 0)

    slope, loss = pl.pallas_call(
        tree_kernel,
        out_shape=[
            jax.ShapeDtypeStruct((samples * rows, LANES), F32),
            jax.ShapeDtypeStruct((1, LANES), F32),
        ],
        name="tree",
    )(mismatch, morton.reshape(rows, LANES))

    spot = jnp.stack([lax.axis_index(name) for name in ("z", "x", "y", "c")]).astype(jnp.int32)
    payload = jax.ShapeDtypeStruct((1040, LANES), F32)
    groups = []
    group = 4
    while group < tiles:
        groups.append(group)
        group = group * 4
    groups.append(tiles)
    patch_prediction_deriv, keep, send = pl.pallas_call(
        functools.partial(backward_kernel, groups=tuple(groups), grad_scale=grad_scale),
        grid_spec=pltpu.PrefetchScalarGridSpec(
            num_scalar_prefetch=1,
            grid=(steps,),
            in_specs=[
                pl.BlockSpec((samples, CB, width), lambda i, _: (0, i, 0)),
                whole((width, width)), whole((1, width)), whole((1, width)),
                whole((samples * rows, LANES)), whole((rows, LANES)),
                whole((16, LANES)), whole((1, LANES)),
            ],
            out_specs=[
                pl.BlockSpec((samples, CB), lambda i, _: (0, i)),
                whole((1040, LANES)), whole((1040, LANES)),
            ],
            scratch_shapes=weight_scratch + [
                pltpu.VMEM((8, LANES), F32),
                pltpu.VMEM((samples, width, CB), F32),
                pltpu.VMEM((width, samples * CB), BF16),
                pltpu.VMEM((width, width), F32),
                pltpu.VMEM((width, LANES), F32),
                pltpu.VMEM((width, LANES), F32),
                pltpu.VMEM((16, LANES), F32),
            ],
        ),
        out_shape=[jax.ShapeDtypeStruct((samples, cells), F32), payload, payload],
        compiler_params=params,
        name="backward",
    )(
        spot, unembed_feature_matrix, weight_in, bias_row, readout_row,
        slope, land_tile, pairs, loss,
    )

    half = keep + lax.ppermute(send, "c", [(0, 1), (1, 0)])
    line = jnp.broadcast_to(half[1024:][None], (16, 16, LANES))
    slots = jnp.concatenate([half[:1024].reshape(16, 64, LANES), line], axis=1)
    own = jnp.sum(lax.all_to_all(slots, ("z", "x"), 0, 0), axis=0)
    for flip in (1, 3):
        own = own + lax.ppermute(own, "y", [(n, n ^ flip) for n in range(4)])
    inner_coefficient_deriv = jnp.concatenate(
        [own[j * 16:(j + 1) * 16] for j in range(width // LANES)], axis=1
    )
    offset_projection_derivs = own[64:72].reshape(2, width)
    penalty_per_example = lax.dynamic_slice_in_dim(
        own[72], lax.axis_index("y") * samples, samples
    ) / (cells * tiles * SHARP)
    return (
        predicted_rainfall,
        patch_prediction_deriv,
        penalty_per_example,
        inner_coefficient_deriv,
        offset_projection_derivs,
    )


def solution(mesh):
    fine = Mesh(mesh.devices.reshape(4, 4, 4, 2), ("y", "z", "x", "c"))
    tile = ("z", "x", "c")
    return jax.shard_map(
        on_device,
        mesh=fine,
        in_specs=(
            P("y", tile, None), P(), P(), P(), P("y", tile), P(tile), P(tile, None),
        ),
        out_specs=(P("y", tile), P("y", tile), P("y"), P(tile, None), P()),
        check_vma=False,
    )
```

time: 327 us -> 112 us (0.34)
  blocking collectives: 129 us -> 17.8 us
  Pallas kernels: 0 us -> 63 us
  matrix products: 57.4 us -> 0 us
  other arithmetic: 51.9 us -> 3.66 us
  local copies, waits for them, and re-layouts: 34.3 us -> 3.13 us
  waiting for transfers between devices: 27.6 us -> 10.4 us
  between operations: 14.3 us -> 0.72 us
    psum x2 -> x0, blocking collectives: 129 us -> none  [the longest x1 64.6 us: on_device(): lax.psum((weight_term, vector_term), ('dp', 'grid'))]
    pallas_call x0 -> x3, Pallas kernels: none -> 63 us  [the longest x1 38.2 us: on_device(): pl.pallas_call(functools.partial(backward_kernel, groups=tuple(groups), g...]
    dot_general x3 -> x0, matrix products: 57.4 us -> none  [the longest x1 29.1 us: on_device(): jnp.dot(flat_rows, weight_in, preferred_element_type=jnp.float32) + bias_in]
    reduce_sum x13 -> x1, other arithmetic: 42.5 us -> 0.04 us  [on_device(): own = jnp.sum(lax.all_to_all(slots, ('z', 'x'), 0, 0), axis=0)]
    psum x1 -> x0, waiting for transfers between devices: 20.6 us -> none  [on_device(): lax.psum((weight_term, vector_term), ('dp', 'grid'))]
    all_to_all x0 -> x1, blocking collectives: none -> 17.8 us  [on_device(): own = jnp.sum(lax.all_to_all(slots, ('z', 'x'), 0, 0), axis=0)]
    gather x1 -> x0, local copies, waits for them, and re-layouts: 12.4 us -> none  [on_device(): sorted_entries = jnp.take(prediction_residual, zorder_line, axis=1)]
    scatter x1 -> x0, local copies, waits for them, and re-layouts: 11.8 us -> none  [on_device(): jnp.zeros_like(steepness).at[:, zorder_line].set(steepness)]
  transfers between devices with their start and end apart: 6 -> 5, of which waited for: 5 -> 5; matrix products, arithmetic and copies ran while one was open for 5% -> 1% of each run, Pallas kernels for 0% -> 4%
where the time goes in v1:
time: 112 us
  Pallas kernels  63 us (56%)
  blocking collectives  17.8 us (16%)
  starting transfers between devices  12.7 us (11%)
  waiting for transfers between devices  10.4 us (9%)
  other arithmetic  3.66 us (3%)
  local copies, waits for them, and re-layouts  3.13 us (3%)
    pallas_call x1, Pallas kernels, on_device(): pl.pallas_call(functools.partial(backward_kernel, groups=tuple(groups), g...  38.2 us
    pallas_call x1, Pallas kernels, on_device(): pl.pallas_call(forward_kernel, grid=(steps,), in_specs=[x_spec, whole((wi...  20.4 us
    all_to_all x1, blocking collectives, on_device(): own = jnp.sum(lax.all_to_all(slots, ('z', 'x'), 0, 0), axis=0)  17.8 us
    all_to_all x1, starting transfers between devices, on_device(): lax.all_to_all(jnp.broadcast_to(core_pair, (16, LANES)), ('z', 'x'), 0, 0)  7.99 us
    ppermute x2, starting transfers between devices, on_device(): own = own + lax.ppermute(own, 'y', [(n, n ^ flip) for n in range(4)])  4.67 us
    ppermute x2, waiting for transfers between devices, on_device(): own = own + lax.ppermute(own, 'y', [(n, n ^ flip) for n in range(4)])  4.62 us
    pallas_call x1, Pallas kernels, on_device(): pl.pallas_call(tree_kernel, out_shape=[jax.ShapeDtypeStruct((samples * ro...  4.51 us
    all_to_all x1, waiting for transfers between devices, on_device(): lax.all_to_all(jnp.broadcast_to(core_pair, (16, LANES)), ('z', 'x'), 0, 0)  2.4 us
  transfers between devices with their start and end apart: 5, of which 5 were waited for; matrix products, arithmetic and copies ran while one was open for 1% of the time, Pallas kernels for 4%

profile of v1, /device:TPU:0, one launch (start us, length us, event | category | flops | bytes accessed | tf_op | source)
XLA Modules:
  0.0 111.6 jit_solution(13154202061648595109)
XLA Ops:
  0.6 1.3 %reshape.42.r_ref = bf16[1,512]{1,0:T(2,128)(2,1)} reshape(bf16[512]{0:T(512)(128)(2,1)} %param.10) | data formatting | bytes 2048 | tf_op jit(solution)/shard_map/reshape | solution.py:285
  1.9 20.4 %forward.1 = (f32[4,4096]{1,0:T(4,128)}, f32[128,128]{1,0:T(8,128)}, f32[1,128]{1,0:T(1,128)}) custom-call(bf16[4,4096,512]{2,1,0:T(8,128)(2,1)} %x_ref.3, bf16[512,512]{1,0:T(8,128)(2,1)} %w_ref.3, f32[1,512]{1,0:T(1,128)} %bitcast.19, bf16[1,512]{1,0:T(2,128)(2,1)} %reshape.42.r_ref, f32[4,4096]{1,0:T(4,128)} %meas_ref.1, s32[1,4096]{1,0:T(1,128)} %bitcast.15), custom_call_target="tpu_custom_call" | custom-call | tf_op jit(solution)/shard_map/forward/pallas_call | solution.py:299
  22.3 0.1 collective-permute-start
  22.4 1.3 %collective-permute-done = f32[1,128]{1,0:T(1,128)S(1)} collective-permute-done((f32[1,128]{1,0:T(1,128)}, f32[1,128]{1,0:T(1,128)S(1)}, u32[]{:S(2)}, u32[]{:S(2)}) %collective-permute-start) | collective-permute-done | bytes 544 | tf_op jit(solution)/shard_map/ppermute | solution.py:317
  23.6 0.7 add_bitcast_fusion
  24.3 0.6 broadcast_in_dim.4
  24.9 8.0 %all-to-all-start = ((f32[16,1,128]{2,1,0:T(1,128)}), f32[16,1,128]{2,1,0:T(1,128)S(1)}, u32[]{:S(2)}, u32[]{:S(2)}) async-start(f32[16,1,128]{2,1,0:T(1,128)} %broadcast_in_dim.4), calls=%async_computation | async-start | bytes 16384 | tf_op jit(solution)/shard_map/all_to_all | solution.py:318
  32.9 0.6 pad_add_fusion.spot_ref
  33.5 4.5 %tree.1 = (f32[128,128]{1,0:T(8,128)}, f32[1,128]{1,0:T(1,128)}) custom-call(f32[128,128]{1,0:T(8,128)} %get-tuple-element.14.mm_ref, s32[32,128]{1,0:T(8,128)} %bitcast.18), custom_call_target="tpu_custom_call" | custom-call | tf_op jit(solution)/shard_map/tree/pallas_call | solution.py:320
  38.0 2.4 %all-to-all-done = f32[16,1,128]{2,1,0:T(1,128)S(1)} async-done(((f32[16,1,128]{2,1,0:T(1,128)}), f32[16,1,128]{2,1,0:T(1,128)S(1)}, u32[]{:S(2)}, u32[]{:S(2)}) %all-to-all-start) | async-done | bytes 8224 | tf_op jit(solution)/shard_map/all_to_all | solution.py:318
  40.4 0.0 copy-start
  40.4 0.6 copy-done
  41.0 38.2 %backward.1 = (f32[4,4096]{1,0:T(4,128)}, f32[1040,128]{1,0:T(8,128)}, f32[1040,128]{1,0:T(8,128)}) custom-call(s32[4]{0:T(128)} %pad_add_fusion.spot_ref, bf16[4,4096,512]{2,1,0:T(8,128)(2,1)} %x_ref.3, bf16[512,512]{1,0:T(8,128)(2,1)} %w_ref.3, f32[1,512]{1,0:T(1,128)} %bitcast.20, bf16[1,512]{1,0:T(2,128)(2,1)} %reshape.42.r_ref, ...), custom_call_target="tpu_custom_call" | custom-call | tf_op jit(solution)/shard_map/backward/pallas_call | solution.py:337
  79.2 0.0 collective-permute-start.1
  79.2 2.1 %collective-permute-done.1 = f32[1040,128]{1,0:T(8,128)S(1)} collective-permute-done((f32[1040,128]{1,0:T(8,128)}, f32[1040,128]{1,0:T(8,128)S(1)}, u32[]{:S(2)}, u32[]{:S(2)}) %collective-permute-start.1) | collective-permute-done | bytes 532512 | tf_op jit(solution)/shard_map/ppermute | solution.py:370
  81.3 1.1 add.19
  82.5 17.8 %all_to_all.13 = f32[16,80,128]{2,1,0:T(8,128)S(1)} all-to-all(f32[16,80,128]{2,1,0:T(8,128)S(1)} %pad_maximum_fusion), channel_id=1, replica_groups=mesh['y'=4,'z'=4,'x'=4,'c'=2] {'z','x'}, dimensions={0} | all-to-all | bytes 1310720 | tf_op jit(solution)/shard_map/all_to_all | solution.py:373
  100.4 1.7 %collective-permute-start.2 = (f32[80,128]{1,0:T(8,128)S(1)}, f32[80,128]{1,0:T(8,128)S(1)}, u32[]{:S(2)}, u32[]{:S(2)}) collective-permute-start(f32[80,128]{1,0:T(8,128)S(1)} %reduce_sum.9), channel_id=1, source_target_pairs={{0,32},{32,0},{64,96},{96,64},{1,33},{33,1},{65,97},{97,65},{2,34}... | collective-permute-start | bytes 122888 | tf_op jit(solution)/shard_map/ppermute | solution.py:375
  102.1 2.4 %collective-permute-done.2 = f32[80,128]{1,0:T(8,128)S(1)} collective-permute-done((f32[80,128]{1,0:T(8,128)S(1)}, f32[80,128]{1,0:T(8,128)S(1)}, u32[]{:S(2)}, u32[]{:S(2)}) %collective-permute-start.2) | collective-permute-done | bytes 40992 | tf_op jit(solution)/shard_map/ppermute | solution.py:375
  104.5 3.0 %collective-permute-start.3 = (f32[80,128]{1,0:T(8,128)S(1)}, f32[80,128]{1,0:T(8,128)S(1)}, u32[]{:S(2)}, u32[]{:S(2)}) collective-permute-start(f32[80,128]{1,0:T(8,128)S(1)} %add.20), channel_id=1, source_target_pairs={{0,96},{32,64},{64,32},{96,0},{1,97},{33,65},{65,33},{97,1},{2,98}... | collective-permute-start | bytes 122888 | tf_op jit(solution)/shard_map/ppermute | solution.py:375
  107.5 2.2 %collective-permute-done.3 = f32[80,128]{1,0:T(8,128)S(1)} collective-permute-done((f32[80,128]{1,0:T(8,128)S(1)}, f32[80,128]{1,0:T(8,128)S(1)}, u32[]{:S(2)}, u32[]{:S(2)}) %collective-permute-start.3) | collective-permute-done | bytes 40992 | tf_op jit(solution)/shard_map/ppermute | solution.py:375
  109.8 0.6 reshape.47
  110.4 0.6 multiply_bitcast_fusion
  110.9 0.6 pad_maximum_fusion.1
  (10 shorter events, 0.2 us)
Async XLA Ops:
  22.3 1.4 %collective-permute-start = (f32[1,128]{1,0:T(1,128)}, f32[1,128]{1,0:T(1,128)S(1)}, u32[]{:S(2)}, u32[]{:S(2)}) collective-permute-start(f32[1,128]{1,0:T(1,128)} %get-tuple-element.16), channel_id=1, source_target_pairs={{0,1},{1,0},{2,3},{3,2},{4,5},{5,4},{6,7},{7,6},{8,9},{9,8},{10,11... | collective-permute-start | bytes 1544 | tf_op jit(solution)/shard_map/ppermute | solution.py:317
  24.9 15.5 %all-to-all-start = ((f32[16,1,128]{2,1,0:T(1,128)}), f32[16,1,128]{2,1,0:T(1,128)S(1)}, u32[]{:S(2)}, u32[]{:S(2)}) async-start(f32[16,1,128]{2,1,0:T(1,128)} %broadcast_in_dim.4), calls=%async_computation | async-start | bytes 16384 | tf_op jit(solution)/shard_map/all_to_all | solution.py:318
  40.4 0.6 copy-start
  79.2 2.1 %collective-permute-start.1 = (f32[1040,128]{1,0:T(8,128)}, f32[1040,128]{1,0:T(8,128)S(1)}, u32[]{:S(2)}, u32[]{:S(2)}) collective-permute-start(f32[1040,128]{1,0:T(8,128)} %get-tuple-element.20), channel_id=1, source_target_pairs={{0,1},{1,0},{2,3},{3,2},{4,5},{5,4},{6,7},{7,6},{8,9},{9,8},{10,11... | collective-permute-start | bytes 1597448 | tf_op jit(solution)/shard_map/ppermute | solution.py:370
  100.4 4.1 %collective-permute-start.2 = (f32[80,128]{1,0:T(8,128)S(1)}, f32[80,128]{1,0:T(8,128)S(1)}, u32[]{:S(2)}, u32[]{:S(2)}) collective-permute-start(f32[80,128]{1,0:T(8,128)S(1)} %reduce_sum.9), channel_id=1, source_target_pairs={{0,32},{32,0},{64,96},{96,64},{1,33},{33,1},{65,97},{97,65},{2,34}... | collective-permute-start | bytes 122888 | tf_op jit(solution)/shard_map/ppermute | solution.py:375
  104.5 5.2 %collective-permute-start.3 = (f32[80,128]{1,0:T(8,128)S(1)}, f32[80,128]{1,0:T(8,128)S(1)}, u32[]{:S(2)}, u32[]{:S(2)}) collective-permute-start(f32[80,128]{1,0:T(8,128)S(1)} %add.20), channel_id=1, source_target_pairs={{0,96},{32,64},{64,32},{96,0},{1,97},{33,65},{65,33},{97,1},{2,98}... | collective-permute-start | bytes 122888 | tf_op jit(solution)/shard_map/ppermute | solution.py:375
